TPU v7x, 256 devices: a whole 4x4x8 slice. The times are simulated.
256 devices in a mesh: row: 32 (over z_lo, x, core), col: 8 (over z_hi, y).
Axes of the slice: x: 4, y: 4, z: 8 (z_hi: 2, z_lo: 4; z = z_hi * 4 + z_lo), core: 2. Of those that a mesh axis runs over, the one named last changes fastest.
Arguments:
- pair: bfloat16 [512, 512, 128], P('row', 'col'), may hold values from -6 to 6
- cotangent: bfloat16 [64, 512, 512], P(None, 'row', 'col'), may hold values from -0.59765625 to 0.59765625
- w_left: bfloat16 [128, 64], replicated, may hold values from -0.5 to 0.5
- w_left_gate: bfloat16 [128, 64], replicated, may hold values from -0.5 to 0.5
- w_right: bfloat16 [128, 64], replicated, may hold values from -0.5 to 0.5
- w_right_gate: bfloat16 [128, 64], replicated, may hold values from -0.5 to 0.5
Outputs:
- pair_gradient: bfloat16 [512, 512, 128], P('row', 'col')
- grad_left: float32 [128, 64], replicated
- grad_left_gate: float32 [128, 64], replicated
- grad_right: float32 [128, 64], replicated
- grad_right_gate: float32 [128, 64], replicated
All inputs are finite; a program needn't handle non-finite values.
Results may differ from a plain program's by a relative error of at most 0.0082.
Values may be sent and summed in bfloat16 or wider, within the bound.
A program may use at most 64 MiB of HBM per device.

v0:
```python
import jax
import jax.numpy as jnp
from jax import lax
from jax.sharding import PartitionSpec as P


def shards(pair, cotangent, w_left, w_left_gate, w_right, w_right_gate):
    pair_f = pair.astype(jnp.float32)
    average = jnp.mean(pair_f, axis=-1, keepdims=True)
    centered_input = pair_f - average
    variance = jnp.mean(centered_input * centered_input, axis=-1, keepdims=True)
    inverse_scale = 1.0 / jnp.sqrt(variance + 1e-05)
    standardized_input = centered_input * inverse_scale
    normalized_input = standardized_input.astype(jnp.bfloat16)
    stacked = jnp.concatenate([w_left, w_left_gate, w_right, w_right_gate], axis=1)
    projected = jnp.einsum(
        "rcd,dh->hrc", normalized_input, stacked, preferred_element_type=jnp.float32
    )
    q_left, p_left, q_right, p_right = jnp.split(projected, 4, axis=0)
    s_left = jax.nn.sigmoid(p_left)
    s_right = jax.nn.sigmoid(p_right)
    left = (s_left * q_left).astype(jnp.bfloat16)
    right = (s_right * q_right).astype(jnp.bfloat16)
    g_chan, left_chan, right_chan = (
        lax.all_to_all(cotangent, "col", split_axis=0, concat_axis=2, tiled=True),
        lax.all_to_all(left, "col", split_axis=0, concat_axis=2, tiled=True),
        lax.all_to_all(right, "col", split_axis=0, concat_axis=2, tiled=True),
    )
    residues = g_chan.shape[2]
    col_block = g_chan
    d_left = jnp.einsum(
        "hij,hjk->hik",
        col_block,
        lax.all_gather(right_chan, "row", axis=1, tiled=True),
        preferred_element_type=jnp.float32,
    )
    col_block = g_chan
    summed = lax.psum_scatter(
        jnp.einsum("hij,hik->jhk", col_block, left_chan, preferred_element_type=jnp.float32),
        "row",
        scatter_dimension=0,
        tiled=True,
    )
    d_right = jnp.transpose(summed, (1, 0, 2))
    d_left_tile, d_right_tile = (
        lax.all_to_all(d_left.astype(jnp.bfloat16), "col", split_axis=2, concat_axis=0, tiled=True),
        lax.all_to_all(
            d_right.astype(jnp.bfloat16), "col", split_axis=2, concat_axis=0, tiled=True
        ),
    )
    grad_l = d_left_tile.astype(jnp.float32)
    grad_r = d_right_tile.astype(jnp.float32)
    e_left = grad_l * s_left
    f_left = grad_l * q_left * s_left * (1.0 - s_left)
    e_right = grad_r * s_right
    f_right = grad_r * q_right * s_right * (1.0 - s_right)
    grads = jnp.concatenate([e_left, f_left, e_right, f_right], axis=0).astype(jnp.bfloat16)
    local_weights = jnp.einsum(
        "rcd,hrc->dh", normalized_input, grads, preferred_element_type=jnp.float32
    )
    total_weights = lax.psum(local_weights, ("row", "col")) / residues
    normalized_gradient = jnp.einsum(
        "hrc,dh->rcd", grads, stacked, preferred_element_type=jnp.float32
    )
    gradient_mean = jnp.mean(normalized_gradient, axis=-1, keepdims=True)
    gradient_input_mean = jnp.mean(normalized_gradient * standardized_input, axis=-1, keepdims=True)
    pair_gradient = (
        (normalized_gradient - gradient_mean - standardized_input * gradient_input_mean)
        * inverse_scale
    ).astype(jnp.bfloat16)
    pieces_w = jnp.split(total_weights, 4, axis=1)
    return (pair_gradient, pieces_w[0], pieces_w[1], pieces_w[2], pieces_w[3])


def solution(mesh):
    in_specs = (P("row", "col", None), P(None, "row", "col"), P(), P(), P(), P())
    out_specs = (P("row", "col", None), P(), P(), P(), P())
    return jax.shard_map(shards, mesh=mesh, in_specs=in_specs, out_specs=out_specs, check_vma=False)
```

profile of v0, /device:TPU:2, one launch (start us, length us, event | category | flops | bytes accessed | tf_op | source)
XLA Modules:
  0.0 579.7 jit_solution(9537658770375944991)
XLA Ops:
  7.2 1.2 convert_reduce_fusion
  8.4 1.3 fusion.10
  9.8 0.8 copy.87
  10.6 0.8 copy.88
  11.4 0.8 copy.89
  12.3 0.8 copy.90
  13.1 1.4 fusion.18
  15.3 21.4 %all_to_all.72 = bf16[8,2,4096]{2,1,0:T(2,128)(2,1)S(1)} all-to-all(bf16[8,2,4096]{2,1,0:T(2,128)(2,1)S(1)} %reshape.47), channel_id=1, replica_groups=mesh['row'=32,'col'=8] {'col'}, dimensions={0} | all-to-all | bytes 262144 | tf_op jit(solution)/shard_map/all_to_all | solution.py:27
  37.1 0.9 all_to_all.56
  38.3 13.0 %all_to_all.73 = bf16[8,2,4096]{2,1,0:T(2,128)(2,1)S(1)} all-to-all(bf16[8,2,4096]{2,1,0:T(2,128)(2,1)S(1)} %reshape.45), channel_id=1, replica_groups=mesh['row'=32,'col'=8] {'col'}, dimensions={0} | all-to-all | bytes 262144 | tf_op jit(solution)/shard_map/all_to_all | solution.py:25
  51.9 43.9 %all-gather.2.cloned.1.call-done = bf16[8,512,512]{2,1,0:T(8,128)(2,1)} async-done(((bf16[8,16,512]{2,1,0:T(8,128)(2,1)}), bf16[8,512,512]{2,1,0:T(8,128)(2,1)}) %all-gather.2.cloned.1.call-update) | async-done | bytes 4194320 | tf_op jit(solution)/shard_map/all_gather | solution.py:34
  95.9 2.8 fusion
  98.7 0.8 copy.94
  99.5 1.1 reshape.49
  100.5 18.0 %all_to_all.74 = bf16[8,2,4096]{2,1,0:T(2,128)(2,1)S(1)} all-to-all(bf16[8,2,4096]{2,1,0:T(2,128)(2,1)S(1)} %reshape.49), channel_id=1, replica_groups=mesh['row'=32,'col'=8] {'col'}, dimensions={0} | all-to-all | bytes 262144 | tf_op jit(solution)/shard_map/all_to_all | solution.py:46
  118.6 0.7 reshape.50
  119.3 0.7 copy.95
  121.4 13.0 %all_to_all.75 = bf16[8,2,4096]{2,1,0:T(2,128)(2,1)S(1)} all-to-all(bf16[8,2,4096]{2,1,0:T(2,128)(2,1)S(1)} %reshape.51), channel_id=1, replica_groups=mesh['row'=32,'col'=8] {'col'}, dimensions={0} | all-to-all | bytes 262144 | tf_op jit(solution)/shard_map/all_to_all | solution.py:26
  135.1 4.5 convolution_bitcast_fusion
  139.6 10.4 %copy.101 = f32[512,8,512]{2,1,0:T(8,128)} copy(f32[512,8,512]{0,2,1:T(8,128)} %convolution_bitcast_fusion) | data formatting | bytes 16777216 | tf_op jit(solution)/shard_map/hij,hik->jhk/transpose | solution.py:39
  150.1 150.5 %reduce-scatter.2.cloned.1.call-done = f32[16,8,512]{2,1,0:T(8,128)} async-done(((f32[512,8,512]{2,1,0:T(8,128)}), f32[16,8,512]{2,1,0:T(8,128)}) %reduce-scatter.2.cloned.1.call-update) | async-done | bytes 262160 | tf_op jit(solution)/shard_map/reduce_scatter | solution.py:38
  300.5 1.0 convert_bitcast_fusion
  301.5 0.8 copy.102
  302.3 1.1 reshape.53
  303.4 16.3 %all_to_all.76 = bf16[8,2,4096]{2,1,0:T(2,128)(2,1)S(1)} all-to-all(bf16[8,2,4096]{2,1,0:T(2,128)(2,1)S(1)} %reshape.53), channel_id=1, replica_groups=mesh['row'=32,'col'=8] {'col'}, dimensions={0} | all-to-all | bytes 262144 | tf_op jit(solution)/shard_map/all_to_all | solution.py:47
  320.4 0.7 copy.103
  322.0 1.5 convolution_bitcast_fusion.1
  323.5 1.0 fusion.21
  324.5 1.3 fusion.9
  325.9 243.5 %all-reduce.2.cloned.1.call-done = f32[128,256]{1,0:T(8,128)} async-done(((f32[128,256]{1,0:T(8,128)}), f32[128,256]{1,0:T(8,128)}) %all-reduce.2.cloned.1.call-update) | async-done | bytes 131088 | tf_op jit(solution)/shard_map/psum | solution.py:61
  569.4 0.9 broadcast_multiply_fusion
  570.4 0.7 copy.110
  (40 shorter events, 7.8 us)
Async XLA Ops:
  7.2 30.9 %copy-start.1 = (bf16[64,16,64]{2,1,0:T(8,128)(2,1)S(1)}, bf16[64,16,64]{2,1,0:T(8,128)(2,1)}, u32[]{:S(2)}) copy-start(bf16[64,16,64]{2,1,0:T(8,128)(2,1)} %param.7) | copy-start | bytes 393220
  7.2 88.7 %all-gather.2.cloned.1.call-start = ((), (), s32[]{:S(2)}) async-start(), calls=%async_computation.6 | async-start | bytes 4325376 | tf_op jit(solution)/shard_map/all_gather | solution.py:34
  38.0 262.5 %reduce-scatter.2.cloned.1.call-start = ((), (), s32[]{:S(2)}) async-start(), calls=%async_computation.7 | async-start | bytes 8650752 | tf_op jit(solution)/shard_map/reduce_scatter | solution.py:38
  150.0 419.4 %all-reduce.2.cloned.1.call-start = ((), (), s32[]{:S(2)}) async-start(), calls=%async_computation.8 | async-start | bytes 262144 | tf_op jit(solution)/shard_map/psum | solution.py:61
  302.3 19.7 %copy-start = (bf16[16,64,128]{2,1,0:T(8,128)(2,1)S(1)}, bf16[16,64,128]{2,1,0:T(8,128)(2,1)}, u32[]{:S(2)}) copy-start(bf16[16,64,128]{2,1,0:T(8,128)(2,1)} %param.6) | copy-start | bytes 786436
Sparse Core Ops, SparseCore 0:
  38.1 57.7 all-gather.1
  150.1 150.3 reduce-scatter.1
  324.7 244.7 all-reduce.1
where the time goes:
time: 581 us; the launch traced here: 580 us
  waiting for transfers between devices  438 us (75%)
  blocking collectives  81.8 us (14%)
  local copies, waits for them, and re-layouts  27.9 us (5%)
  between operations  14 us (2%)
  matrix products  11.3 us (2%)
  other arithmetic  6.66 us (1%)
    psum x1, waiting for transfers between devices, shards(): total_weights = lax.psum(local_weights, ('row', 'col')) / residues  244 us
    reduce_scatter x1, waiting for transfers between devices, shards(): lax.psum_scatter(jnp.einsum('hij,hik->jhk', col_block, left_chan, preferr...  150 us
    all_gather x1, waiting for transfers between devices, shards(): lax.all_gather(right_chan, 'row', axis=1, tiled=True)  43.9 us
    all_to_all x1, blocking collectives, shards(): lax.all_to_all(right, 'col', split_axis=0, concat_axis=2, tiled=True)  21.4 us
    all_to_all x1, blocking collectives, shards(): lax.all_to_all(d_left.astype(jnp.bfloat16), 'col', split_axis=2, concat_a...  18 us
    all_to_all x1, blocking collectives, shards(): lax.all_to_all(d_right.astype(jnp.bfloat16), 'col', split_axis=2, concat_...  16.3 us
    all_to_all x1, blocking collectives, shards(): lax.all_to_all(left, 'col', split_axis=0, concat_axis=2, tiled=True)  13 us
    all_to_all x1, blocking collectives, shards(): lax.all_to_all(cotangent, 'col', split_axis=0, concat_axis=2, tiled=True)  13 us
  transfers between devices with their start and end apart: 3, of which 3 were waited for; matrix products, arithmetic and copies ran while one was open for 0% of the time, Pallas kernels for 0%

commit v1 on v0

--- a/solution.py
+++ b/solution.py
@@ -2,6 +2,7 @@
 import jax.numpy as jnp
 from jax import lax
 from jax.sharding import PartitionSpec as P
+from jax.lax import psum
 
 
 def shards(pair, cotangent, w_left, w_left_gate, w_right, w_right_gate):
@@ -58,7 +59,12 @@
     local_weights = jnp.einsum(
         "rcd,hrc->dh", normalized_input, grads, preferred_element_type=jnp.float32
     )
-    total_weights = lax.psum(local_weights, ("row", "col")) / residues
+
+    def set_steps_all(vals):
+        f_next = psum(vals, axis_name="col")
+        return psum(f_next, axis_name="row")
+
+    total_weights = set_steps_all(local_weights) / residues
     normalized_gradient = jnp.einsum(
         "hrc,dh->rcd", grads, stacked, preferred_element_type=jnp.float32
     )

time: 581 us -> 696 us (1.20)
  waiting for transfers between devices: 438 us -> 549 us
    psum x1 -> x2, waiting for transfers between devices: 244 us -> 355 us  [the longest x1 249 us: set_steps_all(): return psum(f_next, axis_name='row')]
  transfers between devices with their start and end apart: 3 -> 4, of which waited for: 3 -> 4; matrix products, arithmetic and copies ran while one was open for 0% -> 0% of each run, Pallas kernels for 0% -> 0%
where the time goes in v1:
time: 696 us; the launch traced here: 691 us
  waiting for transfers between devices  549 us (79%)
  blocking collectives  81.8 us (12%)
  local copies, waits for them, and re-layouts  27.9 us (4%)
  between operations  14 us (2%)
  matrix products  11.3 us (2%)
    psum x1, waiting for transfers between devices, set_steps_all(): return psum(f_next, axis_name='row')  249 us
    reduce_scatter x1, waiting for transfers between devices, shards(): lax.psum_scatter(jnp.einsum('hij,hik->jhk', col_block, left_chan, preferr...  150 us
    psum x1, waiting for transfers between devices, set_steps_all(): f_next = psum(vals, axis_name='col')  106 us
    all_gather x1, waiting for transfers between devices, shards(): lax.all_gather(right_chan, 'row', axis=1, tiled=True)  43.9 us
    all_to_all x1, blocking collectives, shards(): lax.all_to_all(right, 'col', split_axis=0, concat_axis=2, tiled=True)  21.4 us
    all_to_all x1, blocking collectives, shards(): lax.all_to_all(d_left.astype(jnp.bfloat16), 'col', split_axis=2, concat_a...  18 us
    all_to_all x1, blocking collectives, shards(): lax.all_to_all(d_right.astype(jnp.bfloat16), 'col', split_axis=2, concat_...  16.3 us
  transfers between devices with their start and end apart: 4, of which 4 were waited for; matrix products, arithmetic and copies ran while one was open for 0% of the time, Pallas kernels for 0%

profile of v1, /device:TPU:2, one launch (start us, length us, event | category | flops | bytes accessed | tf_op | source)
XLA Modules:
  0.0 691.2 jit_solution(825061688065287500)
XLA Ops:
  7.2 1.2 convert_reduce_fusion
  8.4 1.3 fusion.10
  9.8 0.8 copy.87
  10.6 0.8 copy.88
  11.4 0.8 copy.89
  12.3 0.8 copy.90
  13.1 1.4 fusion.18
  15.3 21.4 %all_to_all.72 = bf16[8,2,4096]{2,1,0:T(2,128)(2,1)S(1)} all-to-all(bf16[8,2,4096]{2,1,0:T(2,128)(2,1)S(1)} %reshape.47), channel_id=1, replica_groups=mesh['row'=32,'col'=8] {'col'}, dimensions={0} | all-to-all | bytes 262144 | tf_op jit(solution)/shard_map/all_to_all | solution.py:28
  37.1 0.9 all_to_all.56
  38.3 13.0 %all_to_all.73 = bf16[8,2,4096]{2,1,0:T(2,128)(2,1)S(1)} all-to-all(bf16[8,2,4096]{2,1,0:T(2,128)(2,1)S(1)} %reshape.45), channel_id=1, replica_groups=mesh['row'=32,'col'=8] {'col'}, dimensions={0} | all-to-all | bytes 262144 | tf_op jit(solution)/shard_map/all_to_all | solution.py:26
  51.9 43.9 %all-gather.2.cloned.1.call-done = bf16[8,512,512]{2,1,0:T(8,128)(2,1)} async-done(((bf16[8,16,512]{2,1,0:T(8,128)(2,1)}), bf16[8,512,512]{2,1,0:T(8,128)(2,1)}) %all-gather.2.cloned.1.call-update) | async-done | bytes 4194320 | tf_op jit(solution)/shard_map/all_gather | solution.py:35
  95.9 2.8 fusion
  98.7 0.8 copy.94
  99.5 1.1 reshape.49
  100.5 18.0 %all_to_all.74 = bf16[8,2,4096]{2,1,0:T(2,128)(2,1)S(1)} all-to-all(bf16[8,2,4096]{2,1,0:T(2,128)(2,1)S(1)} %reshape.49), channel_id=1, replica_groups=mesh['row'=32,'col'=8] {'col'}, dimensions={0} | all-to-all | bytes 262144 | tf_op jit(solution)/shard_map/all_to_all | solution.py:47
  119.3 0.7 copy.95
  121.4 13.0 %all_to_all.75 = bf16[8,2,4096]{2,1,0:T(2,128)(2,1)S(1)} all-to-all(bf16[8,2,4096]{2,1,0:T(2,128)(2,1)S(1)} %reshape.51), channel_id=1, replica_groups=mesh['row'=32,'col'=8] {'col'}, dimensions={0} | all-to-all | bytes 262144 | tf_op jit(solution)/shard_map/all_to_all | solution.py:27
  135.1 4.5 convolution_bitcast_fusion
  139.6 10.4 %copy.101 = f32[512,8,512]{2,1,0:T(8,128)} copy(f32[512,8,512]{0,2,1:T(8,128)} %convolution_bitcast_fusion) | data formatting | bytes 16777216 | tf_op jit(solution)/shard_map/hij,hik->jhk/transpose | solution.py:40
  150.1 150.5 %reduce-scatter.2.cloned.1.call-done = f32[16,8,512]{2,1,0:T(8,128)} async-done(((f32[512,8,512]{2,1,0:T(8,128)}), f32[16,8,512]{2,1,0:T(8,128)}) %reduce-scatter.2.cloned.1.call-update) | async-done | bytes 262160 | tf_op jit(solution)/shard_map/reduce_scatter | solution.py:39
  300.5 1.0 convert_bitcast_fusion
  301.5 0.8 copy.102
  302.3 1.1 reshape.53
  303.4 16.3 %all_to_all.76 = bf16[8,2,4096]{2,1,0:T(2,128)(2,1)S(1)} all-to-all(bf16[8,2,4096]{2,1,0:T(2,128)(2,1)S(1)} %reshape.53), channel_id=1, replica_groups=mesh['row'=32,'col'=8] {'col'}, dimensions={0} | all-to-all | bytes 262144 | tf_op jit(solution)/shard_map/all_to_all | solution.py:48
  320.4 0.7 copy.103
  322.0 1.5 convolution_bitcast_fusion.1
  323.5 1.0 fusion.21
  324.6 105.9 %all-reduce.3.cloned.1.call-done = f32[128,256]{1,0:T(8,128)} async-done(((f32[128,256]{1,0:T(8,128)}), f32[128,256]{1,0:T(8,128)}) %all-reduce.3.cloned.1.call-update) | async-done | bytes 131088 | tf_op jit(solution)/shard_map/psum | solution.py:64
  430.5 1.3 fusion.9
  431.8 249.1 %all-reduce.5.cloned.1.call-done = f32[128,256]{1,0:T(8,128)} async-done(((f32[128,256]{1,0:T(8,128)}), f32[128,256]{1,0:T(8,128)}) %all-reduce.5.cloned.1.call-update) | async-done | bytes 131088 | tf_op jit(solution)/shard_map/psum | solution.py:65
  680.9 0.9 broadcast_multiply_fusion
  681.9 0.7 copy.110
  (43 shorter events, 8.6 us)
Async XLA Ops:
  7.2 30.9 %copy-start.1 = (bf16[64,16,64]{2,1,0:T(8,128)(2,1)S(1)}, bf16[64,16,64]{2,1,0:T(8,128)(2,1)}, u32[]{:S(2)}) copy-start(bf16[64,16,64]{2,1,0:T(8,128)(2,1)} %param.7) | copy-start | bytes 393220
  7.2 88.7 %all-gather.2.cloned.1.call-start = ((), (), s32[]{:S(2)}) async-start(), calls=%async_computation.6 | async-start | bytes 4325376 | tf_op jit(solution)/shard_map/all_gather | solution.py:35
  38.0 262.5 %reduce-scatter.2.cloned.1.call-start = ((), (), s32[]{:S(2)}) async-start(), calls=%async_computation.7 | async-start | bytes 8650752 | tf_op jit(solution)/shard_map/reduce_scatter | solution.py:39
  150.0 280.5 %all-reduce.3.cloned.1.call-start = ((), (), s32[]{:S(2)}) async-start(), calls=%async_computation.8 | async-start | bytes 262144 | tf_op jit(solution)/shard_map/psum | solution.py:64
  302.3 19.7 %copy-start = (bf16[16,64,128]{2,1,0:T(8,128)(2,1)S(1)}, bf16[16,64,128]{2,1,0:T(8,128)(2,1)}, u32[]{:S(2)}) copy-start(bf16[16,64,128]{2,1,0:T(8,128)(2,1)} %param.6) | copy-start | bytes 786436
  324.5 356.4 %all-reduce.5.cloned.1.call-start = ((), (), s32[]{:S(2)}) async-start(), calls=%async_computation.9 | async-start | bytes 262144 | tf_op jit(solution)/shard_map/psum | solution.py:65
Sparse Core Ops, SparseCore 0:
  38.1 57.7 all-gather.1
  150.1 150.3 reduce-scatter.1
  324.7 105.7 all-reduce.2
  433.0 247.9 all-reduce.4
